TPU v7x, 128 devices: a whole 4x4x4 slice. The times are simulated.
128 devices in a mesh: row: 8 (over z, core), col: 16 (over y, x).
Axes of the slice: x: 4, y: 4, z: 4, core: 2. Of those that a mesh axis runs over, the one named last changes fastest.
Arguments:
- fock: bfloat16 [18432, 18432], P('row', 'col'), may hold values from -6 to 6
- intersection: bfloat16 [18432, 18432], P('row', 'col'), may hold values from -6 to 6
- tile_mask: int32 [2, 144, 144], P(None, 'row', 'col'), may hold values 0 or 1
- coefficients: bfloat16 [256, 7, 20, 128], P(('row', 'col')), may hold values from -0.5 to 0.5
- domains: int32 [256, 7], P(('row', 'col')), may hold values from 0 to 143, all different within a row; in each aligned block of 32 rows (0 to 31, 32 to 63, ...) at most 2 rows name the same one
- neighbours: int32 [256, 2], P(('row', 'col')), may hold values from 0 to 255, all different within a row
- amplitudes: float32 [256, 20, 20], P(('row', 'col')), may hold values from -0.18 to 0.18
Outputs:
- projected: float32 [256, 20, 20], P(('row', 'col'))
Inputs may be any that keep to these rules, and one draw needn't show every extreme that they name: `domains`: each pair names 7 different tiles; among the 32 pairs of one row index (an aligned block of pairs) no tile is named by more than 2 slots. `neighbours`: each pair names 2 different pairs.
All inputs are finite; a program needn't handle non-finite values. No bound on the sum of `tile_mask` on one device may be relied on, other than what follows from the above.
Results may differ from a plain program's by a relative error of at most 0.0041.
Values may be sent and summed in bfloat16 or wider, within the bound.
A program may use at most 256 MiB of HBM per device.

v0:
```python
import jax
import jax.numpy as jnp
from jax import lax
from jax.sharding import PartitionSpec as P

HIGH = lax.Precision.HIGHEST


def in_one_piece(arrays, axis, dim, along):
    both = jnp.concatenate(arrays, axis=along)
    whole, at, done = (lax.all_gather(both, axis, axis=dim, tiled=True), 0, [])
    for a in arrays:
        done.append(lax.slice_in_dim(whole, at, at + a.shape[along], axis=along))
        at += a.shape[along]
    return tuple(done)


def split_up(x, dim, length):
    dims = x.shape
    tiles = x.reshape(*dims[:dim], length, dims[dim] // length, *dims[dim + 1 :])
    return jnp.moveaxis(tiles, dim, 0)


def sent_and_summed(x, axis, dim):
    tiles = split_up(x, dim, lax.axis_size(axis))
    arrived = lax.all_to_all(tiles, axis, split_axis=0, concat_axis=0, tiled=True)
    return arrived.sum(axis=0)


def bucket_slots(coeffs, tiles, base_pair, first_tile, tile_count, capacity):
    group_size, per_pair = tiles.shape
    slot_count = group_size * per_pair
    flat_tiles = tiles.reshape(slot_count)
    position = jnp.arange(slot_count, dtype=jnp.int32)
    pair_owner = base_pair + position // per_pair
    earlier = (flat_tiles[:, None] == flat_tiles[None, :]) & (position[None, :] < position[:, None])
    slot_rank = jnp.sum(earlier.astype(jnp.int32), axis=1)
    wanted = first_tile + jnp.arange(tile_count, dtype=jnp.int32)
    levels = jnp.arange(capacity, dtype=jnp.int32)
    matches = (flat_tiles[None, None, :] == wanted[:, None, None]) & (
        slot_rank[None, None, :] == levels[None, :, None]
    )
    present = jnp.any(matches, axis=2)
    source = jnp.sum(matches.astype(jnp.int32) * position[None, None, :], axis=2)
    flat_coeffs = coeffs.reshape((slot_count,) + coeffs.shape[2:])
    blocks = jnp.take(flat_coeffs, source, axis=0)
    blocks = jnp.where(present[:, :, None, None], blocks, jnp.zeros((), blocks.dtype))
    owners = jnp.where(present, jnp.take(pair_owner, source), -1)
    return (blocks, owners)


def shards(fock, intersection, tile_mask, coefficients, domains, neighbours, amplitudes):
    row_count = lax.axis_size("row")
    col_count = lax.axis_size("col")
    row_index = lax.axis_index("row")
    col_index = lax.axis_index("col")
    pair_dev, per_pair, pno_count, tile_size = coefficients.shape
    link_count = neighbours.shape[1]
    tile_rows = fock.shape[0] // tile_size
    tile_cols = fock.shape[1] // tile_size
    capacity = max(2, pair_dev)
    group_size = pair_dev * col_count
    width = fock.shape[1]
    group_coeffs, group_tiles, group_links = (
        lax.all_gather(coefficients, "col", axis=0, tiled=True),
        *in_one_piece((domains, neighbours), "col", 0, 1),
    )

    def rows_of(coeffs, tiles, base_pair):
        return bucket_slots(coeffs, tiles, base_pair, row_index * tile_rows, tile_rows, capacity)

    def cols_of(coeffs, tiles, base_pair):
        return bucket_slots(coeffs, tiles, base_pair, col_index * tile_cols, tile_cols, capacity)

    all_coeffs, all_tiles, all_links = (
        lax.all_gather(group_coeffs, "row", axis=0, tiled=True),
        lax.all_gather(group_tiles, "row", axis=0, tiled=True),
        lax.all_gather(group_links, "row", axis=0, tiled=True),
    )
    grouped_coeffs = all_coeffs.reshape((row_count, group_size) + all_coeffs.shape[1:])
    grouped_tiles = all_tiles.reshape(row_count, group_size, per_pair)
    bases = jnp.arange(row_count, dtype=jnp.int32) * group_size
    row_blocks, row_owners = jax.vmap(rows_of)(grouped_coeffs, grouped_tiles, bases)
    col_blocks, col_owners = jax.vmap(cols_of)(grouped_coeffs, grouped_tiles, bases)

    def masked(matrix, flags):
        tiled = matrix.reshape(tile_rows, tile_size, tile_cols, tile_size)
        return (tiled * flags.astype(matrix.dtype)[:, None, :, None]).reshape(matrix.shape)

    operator = jnp.concatenate(
        [masked(fock, tile_mask[0]), masked(intersection, tile_mask[1])], axis=1
    )
    operator = operator.reshape(tile_rows, tile_size, 2 * width)
    link_groups = all_links.reshape(row_count, group_size, link_count)
    group_bases = jnp.arange(row_count, dtype=jnp.int32) * group_size

    def one_group(inputs):
        blocks, owners, links_here, base_pair = inputs
        parts = jnp.einsum("tmak,tkw->tmaw", blocks, operator, preferred_element_type=jnp.float32)
        members = base_pair + jnp.arange(group_size, dtype=jnp.int32)
        flat_owners = owners.reshape(-1)
        bucket_count = flat_owners.shape[0]
        flat_parts = parts.reshape(bucket_count, pno_count, 2 * width)
        hits = flat_owners[None, :] == members[:, None]
        order = jnp.cumsum(hits.astype(jnp.int32), axis=1) - 1
        spots = jnp.arange(bucket_count, dtype=jnp.int32)
        total = jnp.zeros((group_size, pno_count, 2 * width), jnp.float32)
        for slot in range(per_pair):
            pick = hits & (order == slot)
            found = jnp.any(pick, axis=1)
            where_at = jnp.sum(pick.astype(jnp.int32) * spots[None, :], axis=1)
            picked = jnp.take(flat_parts, where_at, axis=0)
            total = total + jnp.where(found[:, None, None], picked, jnp.zeros((), jnp.float32))
        left = total.astype(jnp.bfloat16)
        left = left.reshape(group_size, pno_count, 2, tile_cols, tile_size)
        chosen = (col_owners[None, None] == links_here[:, :, None, None, None]).astype(jnp.bfloat16)
        partner = jnp.einsum(
            "qngtm,gtmbk->qntbk", chosen, col_blocks, preferred_element_type=jnp.float32
        ).astype(jnp.bfloat16)
        return jnp.einsum("qamtk,qntbk->qnmab", left, partner, preferred_element_type=jnp.float32)

    terms = lax.map(one_group, (row_blocks, row_owners, link_groups, group_bases))
    flat_terms = terms.reshape(row_count * group_size, -1)
    sectioned = flat_terms.reshape(row_count, col_count, pair_dev, -1)
    sectioned = sent_and_summed(sectioned, "col", 1)
    summed = sent_and_summed(sectioned, "row", 0)
    summed = summed.reshape(pair_dev, link_count, 2, pno_count, pno_count)
    every_amp = lax.all_gather(amplitudes, ("row", "col"), axis=0, tiled=True)
    nearby = jnp.take(every_amp, neighbours, axis=0)
    fock_part = summed[:, :, 0]
    over_part = summed[:, :, 1]
    first = jnp.einsum("pnab,pnbc,pndc->pad", over_part, nearby, fock_part, precision=HIGH)
    second = jnp.einsum("pnab,pnbc,pndc->pad", fock_part, nearby, over_part, precision=HIGH)
    return first + second


def solution(mesh):
    placed = (
        P("row", "col"),
        P("row", "col"),
        P(None, "row", "col"),
        P(("row", "col"), None, None, None),
        P(("row", "col"), None),
        P(("row", "col"), None),
        P(("row", "col"), None, None),
    )
    return jax.shard_map(
        shards, mesh=mesh, in_specs=placed, out_specs=P(("row", "col"), None, None), check_vma=False
    )
```

profile of v0, /device:TPU:1, one launch (start us, length us, event | category | flops | bytes accessed | tf_op | source)
XLA Modules:
  0.0 1144.9 jit_solution(11759695750382023470)
XLA Ops:
  8.1 45.8 %all-gather.6.cloned.1.call-done = bf16[32,7,20,128]{3,1,2,0:T(8,128)(2,1)} async-done(((bf16[2,7,20,128]{3,1,2,0:T(8,128)(2,1)}), bf16[32,7,20,128]{3,1,2,0:T(8,128)(2,1)}) %all-gather.6.cloned.1.call-update) | async-done | bytes 1146896 | tf_op jit(solution)/shard_map/all_gather | solution.py:65
  57.5 17.6 %all-gather = s32[16,2,9]{2,1,0:T(2,128)S(1)} all-gather(s32[1,2,9]{2,1,0:T(2,128)S(1)} %add_bitcast_fusion), channel_id=1, replica_groups=mesh['row'=8,'col'=16] {'col'}, dimensions={0}, use_global_device_ids=true | all-gather | bytes 1224 | tf_op jit(solution)/shard_map/all_gather | solution.py:11
  75.3 21.1 %all-gather.1 = s32[8,32,7]{1,2,0:T(8,128)S(1)} all-gather(s32[1,32,7]{1,2,0:T(8,128)S(1)} %bitcast.147), channel_id=1, replica_groups=mesh['row'=8,'col'=16] {'row'}, dimensions={0}, use_global_device_ids=true | all-gather | bytes 8064 | tf_op jit(solution)/shard_map/all_gather | solution.py:77
  107.7 8.5 copy.140
  122.7 8.6 copy.141
  131.3 8.5 copy.142
  146.3 8.6 copy.143
  154.9 11.4 all-gather.2
  166.8 9.3 pad_maximum_fusion
  176.0 13.8 %copy.171 = bf16[256,7,20,128]{3,2,1,0:T(8,128)(2,1)} copy(bf16[256,7,20,128]{3,0,2,1:T(8,128)(2,1)} %all-gather.8.cloned.1.call-done) | data formatting | bytes 18350080 | tf_op jit(solution)/shard_map/vmap()/reshape;reshape | solution.py:45
  189.8 7.2 gather_fusion.11
  206.4 815.7 %while.12 = (s32[]{:T(128)}, f32[8,32,2,2,20,20]{5,4,3,2,0,1:T(8,128)}, s32[8,9,2]{0,2,1:T(2,128)S(1)}, s32[8,32,2]{1,2,0:T(2,128)}, bf16[8,9,2,20,128]{4,0,2,3,...) while((s32[]{:T(128)}, ...), condition=%wide.region_21.23_spmd, body=%wide.region_5.22_spmd.sunk | while | flops 622367552 | bytes 162233904 | solution.py:122
  220.1 8.9 fusion.72
  229.0 7.1 gather_fusion.1
  236.4 7.2 gather_fusion.2
  243.5 7.1 gather_fusion.3
  250.9 7.1 gather_fusion.4
  265.1 7.1 gather_fusion
  281.2 18.9 %fusion.74 = bf16[32,20,2304]{2,1,0:T(8,128)(2,1)S(1)} fusion(f32[32,20,2304]{2,1,0:T(8,128)} %gather_fusion, f32[32,20,2304]{2,1,0:T(8,128)} %gather_fusion.1, f32[32,20,2304]{2,1,0:T(8,128)} %gather_fusion.2, f32[32,20,2304]{2,1,0:T(8,128)} %gather_fusion.3, f32[32,20,2304]{2,1,0:T(8,128)} %gather_fusion.4, f32[32,20,2304]{2,1,0:T(8,128)} %gather_fusion.5, ...), kind=kLoop, calls=%fused_computation.16.clone.1 | loop fusion | flops 30965760 | bytes 44237248 | tf_op jit(solution)/shard_map/while/body/eval_jaxpr/convert_element_type | solution.py:114
  320.9 8.9 fusion.72
  329.7 7.1 gather_fusion.1
  337.1 7.2 gather_fusion.2
  344.2 7.1 gather_fusion.3
  351.6 7.1 gather_fusion.4
  365.8 7.1 gather_fusion
  381.9 18.9 %fusion.74 = bf16[32,20,2304]{2,1,0:T(8,128)(2,1)S(1)} fusion(f32[32,20,2304]{2,1,0:T(8,128)} %gather_fusion, f32[32,20,2304]{2,1,0:T(8,128)} %gather_fusion.1, f32[32,20,2304]{2,1,0:T(8,128)} %gather_fusion.2, f32[32,20,2304]{2,1,0:T(8,128)} %gather_fusion.3, f32[32,20,2304]{2,1,0:T(8,128)} %gather_fusion.4, f32[32,20,2304]{2,1,0:T(8,128)} %gather_fusion.5, ...), kind=kLoop, calls=%fused_computation.16.clone.1 | loop fusion | flops 30965760 | bytes 44237248 | tf_op jit(solution)/shard_map/while/body/eval_jaxpr/convert_element_type | solution.py:114
  421.6 8.9 fusion.72
  437.8 7.2 gather_fusion.2
  445.0 7.1 gather_fusion.3
  452.3 7.1 gather_fusion.4
  466.6 7.1 gather_fusion
  482.6 18.9 %fusion.74 = bf16[32,20,2304]{2,1,0:T(8,128)(2,1)S(1)} fusion(f32[32,20,2304]{2,1,0:T(8,128)} %gather_fusion, f32[32,20,2304]{2,1,0:T(8,128)} %gather_fusion.1, f32[32,20,2304]{2,1,0:T(8,128)} %gather_fusion.2, f32[32,20,2304]{2,1,0:T(8,128)} %gather_fusion.3, f32[32,20,2304]{2,1,0:T(8,128)} %gather_fusion.4, f32[32,20,2304]{2,1,0:T(8,128)} %gather_fusion.5, ...), kind=kLoop, calls=%fused_computation.16.clone.1 | loop fusion | flops 30965760 | bytes 44237248 | tf_op jit(solution)/shard_map/while/body/eval_jaxpr/convert_element_type | solution.py:114
  522.4 8.9 fusion.72
  538.6 7.2 gather_fusion.2
  545.7 7.1 gather_fusion.3
  553.1 7.1 gather_fusion.4
  567.4 7.1 gather_fusion
  583.4 18.9 %fusion.74 = bf16[32,20,2304]{2,1,0:T(8,128)(2,1)S(1)} fusion(f32[32,20,2304]{2,1,0:T(8,128)} %gather_fusion, f32[32,20,2304]{2,1,0:T(8,128)} %gather_fusion.1, f32[32,20,2304]{2,1,0:T(8,128)} %gather_fusion.2, f32[32,20,2304]{2,1,0:T(8,128)} %gather_fusion.3, f32[32,20,2304]{2,1,0:T(8,128)} %gather_fusion.4, f32[32,20,2304]{2,1,0:T(8,128)} %gather_fusion.5, ...), kind=kLoop, calls=%fused_computation.16.clone.1 | loop fusion | flops 30965760 | bytes 44237248 | tf_op jit(solution)/shard_map/while/body/eval_jaxpr/convert_element_type | solution.py:114
  623.1 8.9 fusion.72
  639.3 7.2 gather_fusion.2
  646.5 7.1 gather_fusion.3
  653.9 7.1 gather_fusion.4
  668.1 7.1 gather_fusion
  684.1 18.9 %fusion.74 = bf16[32,20,2304]{2,1,0:T(8,128)(2,1)S(1)} fusion(f32[32,20,2304]{2,1,0:T(8,128)} %gather_fusion, f32[32,20,2304]{2,1,0:T(8,128)} %gather_fusion.1, f32[32,20,2304]{2,1,0:T(8,128)} %gather_fusion.2, f32[32,20,2304]{2,1,0:T(8,128)} %gather_fusion.3, f32[32,20,2304]{2,1,0:T(8,128)} %gather_fusion.4, f32[32,20,2304]{2,1,0:T(8,128)} %gather_fusion.5, ...), kind=kLoop, calls=%fused_computation.16.clone.1 | loop fusion | flops 30965760 | bytes 44237248 | tf_op jit(solution)/shard_map/while/body/eval_jaxpr/convert_element_type | solution.py:114
  723.9 8.9 fusion.72
  740.1 7.2 gather_fusion.2
  747.2 7.1 gather_fusion.3
  754.6 7.1 gather_fusion.4
  768.9 7.1 gather_fusion
  784.9 18.9 %fusion.74 = bf16[32,20,2304]{2,1,0:T(8,128)(2,1)S(1)} fusion(f32[32,20,2304]{2,1,0:T(8,128)} %gather_fusion, f32[32,20,2304]{2,1,0:T(8,128)} %gather_fusion.1, f32[32,20,2304]{2,1,0:T(8,128)} %gather_fusion.2, f32[32,20,2304]{2,1,0:T(8,128)} %gather_fusion.3, f32[32,20,2304]{2,1,0:T(8,128)} %gather_fusion.4, f32[32,20,2304]{2,1,0:T(8,128)} %gather_fusion.5, ...), kind=kLoop, calls=%fused_computation.16.clone.1 | loop fusion | flops 30965760 | bytes 44237248 | tf_op jit(solution)/shard_map/while/body/eval_jaxpr/convert_element_type | solution.py:114
  824.6 8.9 fusion.72
  840.8 7.2 gather_fusion.2
  848.0 7.1 gather_fusion.3
  855.4 7.1 gather_fusion.4
  869.6 7.1 gather_fusion
  885.6 18.9 %fusion.74 = bf16[32,20,2304]{2,1,0:T(8,128)(2,1)S(1)} fusion(f32[32,20,2304]{2,1,0:T(8,128)} %gather_fusion, f32[32,20,2304]{2,1,0:T(8,128)} %gather_fusion.1, f32[32,20,2304]{2,1,0:T(8,128)} %gather_fusion.2, f32[32,20,2304]{2,1,0:T(8,128)} %gather_fusion.3, f32[32,20,2304]{2,1,0:T(8,128)} %gather_fusion.4, f32[32,20,2304]{2,1,0:T(8,128)} %gather_fusion.5, ...), kind=kLoop, calls=%fused_computation.16.clone.1 | loop fusion | flops 30965760 | bytes 44237248 | tf_op jit(solution)/shard_map/while/body/eval_jaxpr/convert_element_type | solution.py:114
  925.4 8.9 fusion.72
  941.6 7.2 gather_fusion.2
  948.8 7.1 gather_fusion.3
  956.1 7.1 gather_fusion.4
  970.4 7.1 gather_fusion
  986.4 18.9 %fusion.74 = bf16[32,20,2304]{2,1,0:T(8,128)(2,1)S(1)} fusion(f32[32,20,2304]{2,1,0:T(8,128)} %gather_fusion, f32[32,20,2304]{2,1,0:T(8,128)} %gather_fusion.1, f32[32,20,2304]{2,1,0:T(8,128)} %gather_fusion.2, f32[32,20,2304]{2,1,0:T(8,128)} %gather_fusion.3, f32[32,20,2304]{2,1,0:T(8,128)} %gather_fusion.4, f32[32,20,2304]{2,1,0:T(8,128)} %gather_fusion.5, ...), kind=kLoop, calls=%fused_computation.16.clone.1 | loop fusion | flops 30965760 | bytes 44237248 | tf_op jit(solution)/shard_map/while/body/eval_jaxpr/convert_element_type | solution.py:114
  1022.0 9.4 reshape_reshape_reshape.3
  1035.4 89.9 %all_gather.18 = f32[256,20,20]{2,1,0:T(8,128)} all-gather(f32[2,20,20]{2,1,0:T(8,128)S(1)} %copy.122), channel_id=1, replica_groups=mesh['row'=8,'col'=16] {'row','col'}, dimensions={0}, use_global_device_ids=true | all-gather | bytes 412800 | tf_op jit(solution)/shard_map/all_gather | solution.py:128
  (382 shorter events, 395.8 us)
Async XLA Ops:
  6.5 47.4 %all-gather.6.cloned.1.call-start = ((), (), s32[]{:S(2)}) async-start(), calls=%async_computation.2 | async-start | bytes 1392640 | tf_op jit(solution)/shard_map/all_gather | solution.py:65
  8.1 167.9 %all-gather.8.cloned.1.call-start = ((), (), s32[]{:S(2)}) async-start(), calls=%async_computation.3 | async-start | bytes 10321920 | tf_op jit(solution)/shard_map/all_gather | solution.py:76
  106.6 9.7 copy-start.1
  1022.0 13.2 %copy-start = (f32[2,20,20]{2,0,1:T(2,128)S(1)}, f32[2,20,20]{2,0,1:T(2,128)}, u32[]{:S(2)}) copy-start(f32[2,20,20]{2,0,1:T(2,128)} %param.17) | copy-start | bytes 9604
  1022.0 13.2 %copy-start.2 = (s32[2,2]{1,0:T(2,128)S(1)}, s32[2,2]{1,0:T(2,128)}, u32[]{:S(2)}) copy-start(s32[2,2]{1,0:T(2,128)} %param.16) | copy-start | bytes 52
  1031.4 93.9 %all-to-all-start = ((f32[16,8,1,2,1600]{4,1,3,2,0:T(8,128)}), f32[16,8,1,2,1600]{4,1,3,2,0:T(8,128)S(1)}, u32[]{:S(2)}, u32[]{:S(2)}) async-start(f32[16,8,1,2,1600]{4,1,3,2,0:T(8,128)} %bitcast.33), calls=%async_computation | async-start | bytes 3407872 | tf_op jit(solution)/shard_map/all_to_all | solution.py:26
  1126.1 10.0 all-to-all-start.1
Sparse Core Ops, SparseCore 0:
  9.5 44.3 all-gather.5
  56.9 55.0 all-gather.7
where the time goes:
time: 1160 us; the launch traced here: 1140 us
  local copies, waits for them, and re-layouts  564 us (49%)
  other arithmetic  215 us (19%)
  matrix products  144 us (12%)
  blocking collectives  140 us (12%)
  waiting for transfers between devices  48.2 us (4%)
  between operations  13.9 us (1%)
    gather x56, local copies, waits for them, and re-layouts, one_group(): picked = jnp.take(flat_parts, where_at, axis=0)  398 us
    convert_element_type x8, other arithmetic, one_group(): left = total.astype(jnp.bfloat16)  151 us
    all_gather x1, blocking collectives, shards(): every_amp = lax.all_gather(amplitudes, ('row', 'col'), axis=0, tiled=True)  89.9 us
    dot_general x8, matrix products, one_group(): jnp.einsum('tmak,tkw->tmaw', blocks, operator, preferred_element_type=jnp...  70.9 us
    dot_general x8, matrix products, one_group(): jnp.einsum('qamtk,qntbk->qnmab', left, partner, preferred_element_type=jn...  54 us
    all_gather x1, waiting for transfers between devices, shards(): lax.all_gather(coefficients, 'col', axis=0, tiled=True)  45.8 us
    reshape x8, local copies, waits for them, and re-layouts, one_group(): left = left.reshape(group_size, pno_count, 2, tile_cols, tile_size)  38.2 us
  transfers between devices with their start and end apart: 4, of which 2 were waited for; matrix products, arithmetic and copies ran while one was open for 6% of the time, Pallas kernels for 0%

commit v1 on v0

--- a/solution.py
+++ b/solution.py
@@ -125,7 +125,12 @@
     sectioned = sent_and_summed(sectioned, "col", 1)
     summed = sent_and_summed(sectioned, "row", 0)
     summed = summed.reshape(pair_dev, link_count, 2, pno_count, pno_count)
-    every_amp = lax.all_gather(amplitudes, ("row", "col"), axis=0, tiled=True)
+    every_amp = jnp.concatenate(
+        lax.all_to_all(
+            jnp.stack([amplitudes] * lax.axis_size(("row", "col"))), ("row", "col"), 0, 0
+        ),
+        axis=0,
+    )
     nearby = jnp.take(every_amp, neighbours, axis=0)
     fock_part = summed[:, :, 0]
     over_part = summed[:, :, 1]

time: 1160 us -> 1110 us (0.957)
  blocking collectives: 140 us -> 49.5 us
  waiting for transfers between devices: 48.2 us -> 79.5 us
  local copies, waits for them, and re-layouts: 564 us -> 580 us
    all_gather x1 -> x0, blocking collectives: 89.9 us -> none  [shards(): every_amp = lax.all_gather(amplitudes, ('row', 'col'), axis=0, tiled=True)]
    reshape x8, local copies, waits for them, and re-layouts: 38.2 us -> 59.2 us  [one_group(): left = left.reshape(group_size, pno_count, 2, tile_cols, tile_size)]
    all_to_all x2, waiting for transfers between devices: 2.45 us -> 22.8 us  [sent_and_summed(): lax.all_to_all(tiles, axis, split_axis=0, concat_axis=0, tiled=True)]
    convert_element_type x8, other arithmetic: 151 us -> 165 us  [one_group(): left = total.astype(jnp.bfloat16)]
    and x32, other arithmetic: 13.6 us -> 0.27 us  [one_group(): picked = jnp.take(flat_parts, where_at, axis=0)]
    unnamed x12 -> x14, local copies, waits for them, and re-layouts: 18.8 us -> 27.8 us
  transfers between devices with their start and end apart: 4 -> 5, of which waited for: 2 -> 3; matrix products, arithmetic and copies ran while one was open for 6% -> 8% of each run, Pallas kernels for 0% -> 0%
where the time goes in v1:
time: 1110 us; the launch traced here: 1100 us
  local copies, waits for them, and re-layouts  580 us (52%)
  other arithmetic  213 us (19%)
  matrix products  145 us (13%)
  waiting for transfers between devices  79.5 us (7%)
  blocking collectives  49.5 us (4%)
  between operations  14 us (1%)
  starting transfers between devices  13 us (1%)
    gather x56, local copies, waits for them, and re-layouts, one_group(): picked = jnp.take(flat_parts, where_at, axis=0)  399 us
    convert_element_type x8, other arithmetic, one_group(): left = total.astype(jnp.bfloat16)  165 us
    dot_general x8, matrix products, one_group(): jnp.einsum('tmak,tkw->tmaw', blocks, operator, preferred_element_type=jnp...  71.4 us
    reshape x8, local copies, waits for them, and re-layouts, one_group(): left = left.reshape(group_size, pno_count, 2, tile_cols, tile_size)  59.2 us
    dot_general x8, matrix products, one_group(): jnp.einsum('qamtk,qntbk->qnmab', left, partner, preferred_element_type=jn...  54.3 us
    all_gather x1, waiting for transfers between devices, shards(): lax.all_gather(coefficients, 'col', axis=0, tiled=True)  45.7 us
    unnamed x14, local copies, waits for them, and re-layouts  27.8 us
    all_to_all x2, waiting for transfers between devices, sent_and_summed(): lax.all_to_all(tiles, axis, split_axis=0, concat_axis=0, tiled=True)  22.8 us
  transfers between devices with their start and end apart: 5, of which 3 were waited for; matrix products, arithmetic and copies ran while one was open for 8% of the time, Pallas kernels for 0%

profile of v1, /device:TPU:1, one launch (start us, length us, event | category | flops | bytes accessed | tf_op | source)
XLA Modules:
  0.0 1095.8 jit_solution(9345826332467137137)
XLA Ops:
  8.1 45.7 %all-gather.6.cloned.1.call-done = bf16[32,7,20,128]{3,1,2,0:T(8,128)(2,1)} async-done(((bf16[2,7,20,128]{3,1,2,0:T(8,128)(2,1)}), bf16[32,7,20,128]{3,1,2,0:T(8,128)(2,1)}) %all-gather.6.cloned.1.call-update) | async-done | bytes 1146896 | tf_op jit(solution)/shard_map/all_gather | solution.py:65
  57.5 17.6 %all-gather = s32[16,2,9]{2,1,0:T(2,128)S(1)} all-gather(s32[1,2,9]{2,1,0:T(2,128)S(1)} %add_bitcast_fusion), channel_id=1, replica_groups=mesh['row'=8,'col'=16] {'col'}, dimensions={0}, use_global_device_ids=true | all-gather | bytes 1224 | tf_op jit(solution)/shard_map/all_gather | solution.py:11
  75.3 21.1 %all-gather.1 = s32[8,32,7]{1,2,0:T(8,128)S(1)} all-gather(s32[1,32,7]{1,2,0:T(8,128)S(1)} %bitcast.153), channel_id=1, replica_groups=mesh['row'=8,'col'=16] {'row'}, dimensions={0}, use_global_device_ids=true | all-gather | bytes 8064 | tf_op jit(solution)/shard_map/all_gather | solution.py:77
  106.1 8.5 copy.164
  121.1 8.6 copy.165
  129.6 8.5 copy.166
  144.7 8.6 copy.167
  153.3 10.8 all-gather.2
  164.5 9.3 pad_maximum_fusion
  173.8 13.8 %copy.195 = bf16[256,7,20,128]{3,2,1,0:T(8,128)(2,1)} copy(bf16[256,7,20,128]{3,0,2,1:T(8,128)(2,1)} %all-gather.8.cloned.1.call-done) | data formatting | bytes 18350080 | tf_op jit(solution)/shard_map/vmap()/reshape;reshape | solution.py:45
  187.6 7.2 gather_fusion.11
  204.1 808.5 %while.12 = (s32[]{:T(128)}, f32[8,32,2,2,20,20]{5,4,3,2,0,1:T(8,128)}, s32[8,9,2]{0,2,1:T(2,128)S(1)}, s32[8,32,2]{1,2,0:T(2,128)S(1)}, bf16[8,9,2,20,128]{4,0,...) while((s32[]{:T(128)}, ...), condition=%wide.region_21.23_spmd, body=%wide.region_5.22_spmd.sunk | while | flops 622367552 | bytes 162233904 | solution.py:122
  206.5 8.9 fusion.72
  222.8 7.1 gather_fusion.2
  237.2 7.2 gather_fusion.4
  244.4 7.1 gather_fusion.5
  251.5 7.2 gather_fusion
  266.0 20.7 %fusion.74 = bf16[32,20,2304]{2,1,0:T(8,128)(2,1)} fusion(f32[32,20,2304]{2,1,0:T(8,128)} %gather_fusion, f32[32,20,2304]{2,1,0:T(8,128)} %gather_fusion.1, f32[32,20,2304]{2,1,0:T(8,128)} %gather_fusion.2, f32[32,20,2304]{2,1,0:T(8,128)} %gather_fusion.3, f32[32,20,2304]{2,1,0:T(8,128)} %gather_fusion.4, f32[32,20,2304]{2,1,0:T(8,128)} %gather_fusion.5, ...), kind=kLoop, calls=%fused_computation.16.clone.1 | loop fusion | flops 30965760 | bytes 44237248 | tf_op jit(solution)/shard_map/while/body/eval_jaxpr/convert_element_type | solution.py:114
  286.6 7.4 reshape.340
  307.5 8.9 fusion.72
  338.2 7.2 gather_fusion.4
  345.4 7.1 gather_fusion.5
  352.5 7.2 gather_fusion
  366.9 20.7 %fusion.74 = bf16[32,20,2304]{2,1,0:T(8,128)(2,1)} fusion(f32[32,20,2304]{2,1,0:T(8,128)} %gather_fusion, f32[32,20,2304]{2,1,0:T(8,128)} %gather_fusion.1, f32[32,20,2304]{2,1,0:T(8,128)} %gather_fusion.2, f32[32,20,2304]{2,1,0:T(8,128)} %gather_fusion.3, f32[32,20,2304]{2,1,0:T(8,128)} %gather_fusion.4, f32[32,20,2304]{2,1,0:T(8,128)} %gather_fusion.5, ...), kind=kLoop, calls=%fused_computation.16.clone.1 | loop fusion | flops 30965760 | bytes 44237248 | tf_op jit(solution)/shard_map/while/body/eval_jaxpr/convert_element_type | solution.py:114
  387.6 7.4 reshape.340
  408.5 8.9 fusion.72
  439.2 7.2 gather_fusion.4
  446.4 7.1 gather_fusion.5
  453.5 7.2 gather_fusion
  467.9 20.7 %fusion.74 = bf16[32,20,2304]{2,1,0:T(8,128)(2,1)} fusion(f32[32,20,2304]{2,1,0:T(8,128)} %gather_fusion, f32[32,20,2304]{2,1,0:T(8,128)} %gather_fusion.1, f32[32,20,2304]{2,1,0:T(8,128)} %gather_fusion.2, f32[32,20,2304]{2,1,0:T(8,128)} %gather_fusion.3, f32[32,20,2304]{2,1,0:T(8,128)} %gather_fusion.4, f32[32,20,2304]{2,1,0:T(8,128)} %gather_fusion.5, ...), kind=kLoop, calls=%fused_computation.16.clone.1 | loop fusion | flops 30965760 | bytes 44237248 | tf_op jit(solution)/shard_map/while/body/eval_jaxpr/convert_element_type | solution.py:114
  488.6 7.4 reshape.340
  509.6 8.9 fusion.72
  540.3 7.2 gather_fusion.4
  547.4 7.1 gather_fusion.5
  554.6 7.2 gather_fusion
  569.0 20.7 %fusion.74 = bf16[32,20,2304]{2,1,0:T(8,128)(2,1)} fusion(f32[32,20,2304]{2,1,0:T(8,128)} %gather_fusion, f32[32,20,2304]{2,1,0:T(8,128)} %gather_fusion.1, f32[32,20,2304]{2,1,0:T(8,128)} %gather_fusion.2, f32[32,20,2304]{2,1,0:T(8,128)} %gather_fusion.3, f32[32,20,2304]{2,1,0:T(8,128)} %gather_fusion.4, f32[32,20,2304]{2,1,0:T(8,128)} %gather_fusion.5, ...), kind=kLoop, calls=%fused_computation.16.clone.1 | loop fusion | flops 30965760 | bytes 44237248 | tf_op jit(solution)/shard_map/while/body/eval_jaxpr/convert_element_type | solution.py:114
  589.7 7.4 reshape.340
  610.6 8.9 fusion.72
  641.3 7.2 gather_fusion.4
  648.5 7.1 gather_fusion.5
  655.6 7.2 gather_fusion
  670.0 20.7 %fusion.74 = bf16[32,20,2304]{2,1,0:T(8,128)(2,1)} fusion(f32[32,20,2304]{2,1,0:T(8,128)} %gather_fusion, f32[32,20,2304]{2,1,0:T(8,128)} %gather_fusion.1, f32[32,20,2304]{2,1,0:T(8,128)} %gather_fusion.2, f32[32,20,2304]{2,1,0:T(8,128)} %gather_fusion.3, f32[32,20,2304]{2,1,0:T(8,128)} %gather_fusion.4, f32[32,20,2304]{2,1,0:T(8,128)} %gather_fusion.5, ...), kind=kLoop, calls=%fused_computation.16.clone.1 | loop fusion | flops 30965760 | bytes 44237248 | tf_op jit(solution)/shard_map/while/body/eval_jaxpr/convert_element_type | solution.py:114
  690.7 7.4 reshape.340
  711.6 8.9 fusion.72
  742.3 7.2 gather_fusion.4
  749.5 7.1 gather_fusion.5
  756.6 7.2 gather_fusion
  771.1 20.7 %fusion.74 = bf16[32,20,2304]{2,1,0:T(8,128)(2,1)} fusion(f32[32,20,2304]{2,1,0:T(8,128)} %gather_fusion, f32[32,20,2304]{2,1,0:T(8,128)} %gather_fusion.1, f32[32,20,2304]{2,1,0:T(8,128)} %gather_fusion.2, f32[32,20,2304]{2,1,0:T(8,128)} %gather_fusion.3, f32[32,20,2304]{2,1,0:T(8,128)} %gather_fusion.4, f32[32,20,2304]{2,1,0:T(8,128)} %gather_fusion.5, ...), kind=kLoop, calls=%fused_computation.16.clone.1 | loop fusion | flops 30965760 | bytes 44237248 | tf_op jit(solution)/shard_map/while/body/eval_jaxpr/convert_element_type | solution.py:114
  791.7 7.4 reshape.340
  812.6 8.9 fusion.72
  843.3 7.2 gather_fusion.4
  850.5 7.1 gather_fusion.5
  857.6 7.2 gather_fusion
  872.1 20.7 %fusion.74 = bf16[32,20,2304]{2,1,0:T(8,128)(2,1)} fusion(f32[32,20,2304]{2,1,0:T(8,128)} %gather_fusion, f32[32,20,2304]{2,1,0:T(8,128)} %gather_fusion.1, f32[32,20,2304]{2,1,0:T(8,128)} %gather_fusion.2, f32[32,20,2304]{2,1,0:T(8,128)} %gather_fusion.3, f32[32,20,2304]{2,1,0:T(8,128)} %gather_fusion.4, f32[32,20,2304]{2,1,0:T(8,128)} %gather_fusion.5, ...), kind=kLoop, calls=%fused_computation.16.clone.1 | loop fusion | flops 30965760 | bytes 44237248 | tf_op jit(solution)/shard_map/while/body/eval_jaxpr/convert_element_type | solution.py:114
  892.8 7.4 reshape.340
  913.7 8.9 fusion.72
  944.4 7.2 gather_fusion.4
  951.6 7.1 gather_fusion.5
  958.7 7.2 gather_fusion
  973.1 20.7 %fusion.74 = bf16[32,20,2304]{2,1,0:T(8,128)(2,1)} fusion(f32[32,20,2304]{2,1,0:T(8,128)} %gather_fusion, f32[32,20,2304]{2,1,0:T(8,128)} %gather_fusion.1, f32[32,20,2304]{2,1,0:T(8,128)} %gather_fusion.2, f32[32,20,2304]{2,1,0:T(8,128)} %gather_fusion.3, f32[32,20,2304]{2,1,0:T(8,128)} %gather_fusion.4, f32[32,20,2304]{2,1,0:T(8,128)} %gather_fusion.5, ...), kind=kLoop, calls=%fused_computation.16.clone.1 | loop fusion | flops 30965760 | bytes 44237248 | tf_op jit(solution)/shard_map/while/body/eval_jaxpr/convert_element_type | solution.py:114
  993.8 7.4 reshape.340
  1012.7 9.4 reshape_reshape_reshape.3
  1032.0 22.8 %all-to-all-done.1 = f32[16,8,1,2,1600]{4,1,3,2,0:T(8,128)} async-done(((f32[16,8,1,2,1600]{4,1,3,2,0:T(8,128)}), f32[16,8,1,2,1600]{4,1,3,2,0:T(8,128)}, u32[]{:S(2)}, u32[]{:S(2)}) %all-to-all-start.1) | async-done | bytes 1638432 | tf_op jit(solution)/shard_map/all_to_all | solution.py:26
  1061.5 11.0 %all-to-all-done = f32[128,1,800]{2,1,0:T(1,128)S(1)} async-done(((f32[128,1,800]{2,1,0:T(1,128)}), f32[128,1,800]{2,1,0:T(1,128)S(1)}, u32[]{:S(2)}, u32[]{:S(2)}) %all-to-all-start) | async-done | bytes 409632 | tf_op jit(solution)/shard_map/all_to_all | solution.py:129
  (388 shorter events, 402.8 us)
Async XLA Ops:
  6.5 1020.1 %copy-start = (f32[2,20,20]{2,0,1:T(2,128)S(1)}, f32[2,20,20]{2,0,1:T(2,128)}, u32[]{:S(2)}) copy-start(f32[2,20,20]{2,0,1:T(2,128)} %param.17) | copy-start | bytes 9604
  6.5 47.4 %all-gather.6.cloned.1.call-start = ((), (), s32[]{:S(2)}) async-start(), calls=%async_computation.3 | async-start | bytes 1392640 | tf_op jit(solution)/shard_map/all_gather | solution.py:65
  8.1 165.7 %all-gather.8.cloned.1.call-start = ((), (), s32[]{:S(2)}) async-start(), calls=%async_computation.4 | async-start | bytes 10321920 | tf_op jit(solution)/shard_map/all_gather | solution.py:76
  105.6 9.0 copy-start.1
  1022.1 37.1 %copy-start.2 = (s32[2,2]{1,0:T(2,128)S(1)}, s32[2,2]{1,0:T(2,128)}, u32[]{:S(2)}) copy-start(s32[2,2]{1,0:T(2,128)} %param.16) | copy-start | bytes 52
  1022.1 32.7 %all-to-all-start.1 = ((f32[16,8,1,2,1600]{4,1,3,2,0:T(8,128)}), f32[16,8,1,2,1600]{4,1,3,2,0:T(8,128)}, u32[]{:S(2)}, u32[]{:S(2)}) async-start(f32[16,8,1,2,1600]{4,1,3,2,0:T(8,128)} %bitcast.34), calls=%async_computation.1 | async-start | bytes 3407872 | tf_op jit(solution)/shard_map/all_to_all | solution.py:26
  1054.7 17.8 %all-to-all-start = ((f32[128,1,800]{2,1,0:T(1,128)}), f32[128,1,800]{2,1,0:T(1,128)S(1)}, u32[]{:S(2)}, u32[]{:S(2)}) async-start(f32[128,1,800]{2,1,0:T(1,128)} %reshape.309), calls=%async_computation | async-start | bytes 917504 | tf_op jit(solution)/shard_map/all_to_all | solution.py:129
  1072.5 14.5 %all-to-all-start.2 = ((f32[8,1,1,2,1600]{4,3,2,1,0:T(2,128)}), f32[8,1,1,2,1600]{4,3,2,1,0:T(2,128)S(1)}, u32[]{:S(2)}, u32[]{:S(2)}) async-start(f32[8,1,1,2,1600]{4,3,2,1,0:T(2,128)} %copy.172), calls=%async_computation.2 | async-start | bytes 212992 | tf_op jit(solution)/shard_map/all_to_all | solution.py:26
Sparse Core Ops, SparseCore 0:
  9.5 44.3 all-gather.5
  56.9 55.0 all-gather.7
